TPU v7x, 256 devices: a whole 4x4x8 slice. The times are simulated.
256 devices in a mesh: row: 8 (over z), col: 32 (over x, y, core).
Axes of the slice: x: 4, y: 4, z: 8, core: 2. Of those that a mesh axis runs over, the one named last changes fastest.
Arguments:
- three_index: float32 [256, 512, 1024], P('col', None, 'row'), may hold values from -1.2 to 1.2
- occ_energy: float32 [256], replicated, may hold values from -2 to -0.5
- vir_energy: float32 [512], replicated, may hold values from 0.5 to 3
- block_mask: int32 [256, 8, 16], replicated, may hold values from 0 to 1, as said below
- pair_list: int32 [256, 4], P('col'), may hold values from -1 to 3, as said below
Outputs:
- response_density: float32 [256, 512, 1024], P('col', None, 'row')
- virtual_density: float32 [512, 512], replicated
Inputs may be any that keep to these rules, and one draw needn't show every extreme that they name: `block_mask`: each orbital keeps between 32 and 64 of its 128 blocks; some orbital keeps exactly 64. `pair_list`: in each row the live entries come first and are distinct, then -1; every orbital lists at least one partner class; some orbital lists 4.
All inputs are finite; a program needn't handle non-finite values.
Results may differ from a plain program's by a relative error of at most 0.0003.
Values sent between devices are 32-bit elements; how exact they have to be, the bound alone decides.
A program may use at most 128 MiB of HBM per device.

v0:
```python
import jax
import jax.numpy as jnp
from jax import lax
from jax.sharding import PartitionSpec as P

NVIR = 512
NAUX = 1024
BLOCK = 64
STEPS = 2
PAIRS_DEV = 4


def spread(block, axis, holder):
    block = jnp.where(lax.axis_index(axis) == holder, block, jnp.zeros_like(block))
    return lax.psum(block, axis)


def expand_mask(block_rows):
    widened = jnp.repeat(block_rows.astype(jnp.float32), BLOCK, axis=-2)
    return jnp.repeat(widened, BLOCK, axis=-1)


def pair_terms(own_rows, partner, energy_own, energy_partner, virtual):
    cross_term = lax.dot_general(
        own_rows,
        partner,
        (((1,), (1,)), ((), ())),
        precision=lax.Precision.HIGHEST,
        preferred_element_type=jnp.float32,
    )
    denominator = energy_own + energy_partner - virtual[:, None] - virtual[None, :]
    amplitude = cross_term / denominator
    weighted = 2.0 * amplitude - amplitude.T
    response = jnp.dot(
        weighted, partner, precision=lax.Precision.HIGHEST, preferred_element_type=jnp.float32
    )
    virt_density = lax.dot_general(
        weighted,
        amplitude,
        (((1,), (1,)), ((), ())),
        precision=lax.Precision.HIGHEST,
        preferred_element_type=jnp.float32,
    )
    return (response, virt_density)


def on_device(three_index, occ_energy, vir_energy, block_mask, pair_list):
    row_index = lax.axis_index("row")
    col_index = lax.axis_index("col")
    row_count = lax.axis_size("row")
    col_count = lax.axis_size("col")
    own_orbital = col_index * row_count + row_index
    gathered = lax.all_to_all(three_index, "row", split_axis=0, concat_axis=2, tiled=True)
    own_rows = gathered[0] * expand_mask(block_mask[own_orbital])
    panels = []
    for owner_step in range(STEPS):
        first_root = 2 * owner_step
        second_root = first_root + 1
        panels.append(spread(own_rows, "col", first_root))
        panels.append(spread(own_rows, "col", second_root))
    stacked = jnp.stack(panels)
    energy_own = occ_energy[own_orbital]
    response_sum = jnp.zeros((NVIR, NAUX), jnp.float32)
    density_sum = jnp.zeros((NVIR, NVIR), jnp.float32)
    for slot_index in range(PAIRS_DEV):
        listed = pair_list[row_index, slot_index]
        panel_index = jnp.maximum(listed, 0)
        partner = stacked[panel_index]
        energy_partner = occ_energy[panel_index * row_count + row_index]
        live = (listed >= 0).astype(jnp.float32)
        response, virt_density = pair_terms(
            own_rows, partner, energy_own, energy_partner, vir_energy
        )
        response = live * response
        virt_density = live * virt_density
        response_sum = response_sum + response
        density_sum = density_sum + virt_density
    returned = lax.all_to_all(response_sum[None], "row", split_axis=2, concat_axis=0, tiled=True)
    total = lax.psum(density_sum, ("row", "col"))
    return (returned, total / (row_count * col_count))


def solution(mesh):
    placed = (P("col", None, "row"), P(), P(), P(), P("col", None))
    return jax.shard_map(
        on_device,
        mesh=mesh,
        in_specs=placed,
        out_specs=(P("col", None, "row"), P()),
        check_vma=False,
    )
```

profile of v0, /device:TPU:2, one launch (start us, length us, event | category | flops | bytes accessed | tf_op | source)
XLA Modules:
  0.0 567.0 jit_solution(334607822717897980)
XLA Ops:
  7.2 2.9 copy.21
  10.1 8.5 %all-to-all-start = ((f32[8,512,128]{1,2,0:T(8,128)}), f32[8,512,128]{1,2,0:T(8,128)S(1)}, u32[]{:S(2)}, u32[]{:S(2)}) async-start(f32[8,512,128]{1,2,0:T(8,128)} %copy.21), calls=%async_computation | async-start | bytes 4194304 | tf_op jit(solution)/shard_map/all_to_all | solution.py:53
  19.1 50.7 %all-to-all-done = f32[8,512,128]{1,2,0:T(8,128)S(1)} async-done(((f32[8,512,128]{1,2,0:T(8,128)}), f32[8,512,128]{1,2,0:T(8,128)S(1)}, u32[]{:S(2)}, u32[]{:S(2)}) %all-to-all-start) | async-done | bytes 2097184 | tf_op jit(solution)/shard_map/all_to_all | solution.py:53
  69.8 3.9 select_bitcast_fusion
  86.0 2.2 bitcast_multiply_fusion.1
  88.2 111.9 %all-reduce.6.cloned.1.call-done = (f32[1,512,1024]{1,2,0:T(8,128)}, f32[1,512,1024]{1,2,0:T(8,128)}, f32[1,512,1024]{1,2,0:T(8,128)}, f32[1,512,1024]{1,2,0:T(8,128)}) async-done(((f32[1,512,1024]{1,2,0:T(8,128)}, f32[1,512,1024]{1,2,0:T(8,128)}, f32[1,512,1024]{1,2,0:T(8,128)}, f32[1,512,1024]{1,2,0:T(8,128)}), (f32[1,512,1024]{1,2,0:T(8,128)}, f32[1,512,1024]{1,2,0:T(8,128)}, f32[1,512,1024]{1,2,0:T(8,128)}, ...) | async-done | bytes 8388624 | tf_op jit(solution)/shard_map/psum | solution.py:15
  205.8 3.5 fusion.2
  209.3 4.6 fusion.6
  213.9 4.9 fusion.10
  218.7 4.5 fusion.14
  223.3 2.7 copy.24
  229.9 9.2 %fusion.8 = f32[512,1024]{1,0:T(8,128)S(1)} fusion(f32[4,512,1024]{1,2,0:T(8,128)} %copy-done.2, s32[]{:T(128)} %bitcast.18, f32[512,512]{1,0:T(8,128)S(1)} %copy-done.5, f32[512]{0:T(512)S(1)} %get-tuple-element.11, f32[512]{0:T(512)S(1)} %copy-done.19, f32[512,512]{0,1:T(8,128)} %copy.25), kind=kOutput, calls=%fused_computation.9 | convolution fusion | flops 3222798336 | bytes 6300160 | tf_op jit(solution)/shard_map/dot_general | solution.py:34
  239.1 8.7 %fusion.4 = f32[512,1024]{1,0:T(8,128)S(1)} fusion(f32[4,512,1024]{1,2,0:T(8,128)} %copy-done.2, s32[]{:T(128)} %bitcast.23, f32[512,512]{1,0:T(8,128)S(1)} %copy-done.3, f32[512]{0:T(512)S(1)} %get-tuple-element.13, f32[512]{0:T(512)S(1)} %copy-done.19, f32[512,512]{0,1:T(8,128)S(1)} %copy-done.13), kind=kOutput, calls=%fused_computation.5 | convolution fusion | flops 3222798336 | bytes 6300160 | tf_op jit(solution)/shard_map/dot_general | solution.py:34
  247.9 7.2 %fusion = f32[512,1024]{1,0:T(8,128)S(1)} fusion(f32[4,512,1024]{1,2,0:T(8,128)S(1)} %bitcast.112, s32[]{:T(128)} %bitcast.28, f32[512,512]{1,0:T(8,128)S(1)} %fusion.2, f32[512]{0:T(512)S(1)} %get-tuple-element.12, f32[512]{0:T(512)S(1)} %copy-done.19, f32[512,512]{0,1:T(8,128)S(1)} %copy-done.11), kind=kOutput, calls=%fused_computation.1 | convolution fusion | flops 3222798336 | bytes 6299652 | tf_op jit(solution)/shard_map/dot_general | solution.py:34
  255.1 7.2 %add_bitcast_fusion = f32[1,512,1024]{2,1,0:T(8,128)S(1)} fusion(f32[512,1024]{1,0:T(8,128)S(1)} %fusion, f32[512,1024]{1,0:T(8,128)S(1)} %fusion.4, f32[512,1024]{1,0:T(8,128)S(1)} %fusion.8, f32[4,512,1024]{1,2,0:T(8,128)S(1)} %bitcast.112, s32[]{:T(128)} %bitcast.13, f32[]{:T(128)} %bitcast.27, f32[]{:T(128)} %bitcast.22, f32[]{:T(128)} %bitcast.17, ...), kind=kOutput, calls=%fused_computation.18 | convolution fusion | flops 3226468352 | bytes 12591124 | tf_op jit(solution)/shard_map/dot_general | solution.py:34
  262.3 3.7 copy.28
  266.0 7.0 %all-to-all-start.1 = ((f32[1,512,1024]{1,0,2:T(1,128)}), f32[1,512,1024]{1,0,2:T(1,128)S(1)}, u32[]{:S(2)}, u32[]{:S(2)}) async-start(f32[1,512,1024]{1,0,2:T(1,128)} %copy.28), calls=%async_computation.1 | async-start | bytes 4194304 | tf_op jit(solution)/shard_map/all_to_all | solution.py:78
  273.3 4.5 convolution_multiply_fusion.3
  277.8 2.5 fusion.28
  280.4 2.5 fusion.27
  282.9 3.5 fusion.26
  286.4 267.5 %all-reduce.4.cloned.1.call-done = f32[512,512]{1,0:T(8,128)} async-done(((f32[512,512]{1,0:T(8,128)}), f32[512,512]{1,0:T(8,128)}) %all-reduce.4.cloned.1.call-update) | async-done | bytes 1048592 | tf_op jit(solution)/shard_map/psum | solution.py:79
  553.9 2.3 broadcast_multiply_fusion
  556.2 3.6 copy.29
  (67 shorter events, 12.7 us)
Async XLA Ops:
  7.2 11.5 %copy-start = (s32[256,8,16]{0,2,1:T(8,128)S(1)}, s32[256,8,16]{0,2,1:T(8,128)}, u32[]{:S(2)}) copy-start(s32[256,8,16]{0,2,1:T(8,128)} %param.8) | copy-start | bytes 393220
  10.1 59.7 %all-to-all-start = ((f32[8,512,128]{1,2,0:T(8,128)}), f32[8,512,128]{1,2,0:T(8,128)S(1)}, u32[]{:S(2)}, u32[]{:S(2)}) async-start(f32[8,512,128]{1,2,0:T(8,128)} %copy.21), calls=%async_computation | async-start | bytes 4194304 | tf_op jit(solution)/shard_map/all_to_all | solution.py:53
  18.6 181.6 %all-reduce.6.cloned.1.call-start = ((), (), s32[]{:S(2)}) async-start(), calls=%async_computation.3 | async-start | bytes 16777216 | tf_op jit(solution)/shard_map/psum | solution.py:15
  69.8 4.0 copy-start.1
  73.7 6.4 %copy-start.17 = (f32[256]{0:T(256)S(1)}, f32[256]{0:T(256)}, u32[]{:S(2)}) copy-start(f32[256]{0:T(256)} %param.6) | copy-start | bytes 3076
  73.7 12.0 %copy-start.19 = (f32[512]{0:T(512)S(1)}, f32[512]{0:T(512)}, u32[]{:S(2)}) copy-start(f32[512]{0:T(512)} %param.7) | copy-start | bytes 6148
  200.2 2.2 copy-start.10
  202.4 1.6 copy-start.9
  205.8 13.0 %copy-start.2 = (f32[4,512,1024]{1,2,0:T(8,128)}, f32[4,512,1024]{1,2,0:T(8,128)S(1)}, u32[]{:S(2)}) copy-start(f32[4,512,1024]{1,2,0:T(8,128)S(1)} %constant_dynamic-update-slice_fusion) | copy-start | bytes 25165828
  223.2 2.7 copy-start.5
  223.2 4.0 copy-start.3
  229.9 9.2 %copy-start.13 = (f32[512,512]{0,1:T(8,128)S(1)}, f32[512,512]{0,1:T(8,128)}, u32[]{:S(2)}) copy-start(f32[512,512]{0,1:T(8,128)} %copy.26) | copy-start | bytes 3145732
  229.9 17.9 %slice-start = ((s8[8388608]{0:T(1024)(128)(4,1)}), s8[4194304]{0:T(1024)(128)(4,1)S(1)}, s32[]{:S(2)}) async-start(s8[8388608]{0:T(1024)(128)(4,1)} %bitcast.111), calls=%async_computation.4 | async-start | bytes 8388608
  239.1 8.7 %slice-start.1 = ((s8[8388608]{0:T(1024)(128)(4,1)}), s8[4194304]{0:T(1024)(128)(4,1)S(1)}, s32[]{:S(2)}) async-start(s8[8388608]{0:T(1024)(128)(4,1)} %bitcast.111), calls=%async_computation.5 | async-start | bytes 8388608
  239.1 8.7 %copy-start.11 = (f32[512,512]{0,1:T(8,128)S(1)}, f32[512,512]{0,1:T(8,128)}, u32[]{:S(2)}) copy-start(f32[512,512]{0,1:T(8,128)} %copy.27) | copy-start | bytes 3145732
  247.9 7.2 %copy-start.7 = (f32[512,512]{1,0:T(8,128)S(1)}, f32[512,512]{1,0:T(8,128)}, u32[]{:S(2)}) copy-start(f32[512,512]{1,0:T(8,128)} %fusion.14) | copy-start | bytes 3145732
  247.9 7.2 %copy-start.16 = (f32[512,512]{0,1:T(8,128)S(1)}, f32[512,512]{0,1:T(8,128)}, u32[]{:S(2)}) copy-start(f32[512,512]{0,1:T(8,128)} %copy.24) | copy-start | bytes 3145732
  266.0 290.2 %all-to-all-start.1 = ((f32[1,512,1024]{1,0,2:T(1,128)}), f32[1,512,1024]{1,0,2:T(1,128)S(1)}, u32[]{:S(2)}, u32[]{:S(2)}) async-start(f32[1,512,1024]{1,0,2:T(1,128)} %copy.28), calls=%async_computation.1 | async-start | bytes 4194304 | tf_op jit(solution)/shard_map/all_to_all | solution.py:78
  273.0 280.9 %all-reduce.4.cloned.1.call-start = ((), (), s32[]{:S(2)}) async-start(), calls=%async_computation.2 | async-start | bytes 2097152 | tf_op jit(solution)/shard_map/psum | solution.py:79
  273.3 4.5 copy-start.6
  273.3 4.5 copy-start.15
  277.8 2.5 copy-start.4
  277.8 2.5 copy-start.14
  280.3 2.5 copy-start.12
  (2 other events, 2.3 us)
Sparse Core Ops, SparseCore 0:
  73.9 126.2 all-reduce.5
  286.5 267.3 all-reduce.3
where the time goes:
time: 576 us; the launch traced here: 567 us
  waiting for transfers between devices  430 us (75%)
  matrix products  62.6 us (11%)
  local copies, waits for them, and re-layouts  25.2 us (4%)
  between operations  24.9 us (4%)
  starting transfers between devices  15.8 us (3%)
  other arithmetic  8.42 us (1%)
    psum x1, waiting for transfers between devices, on_device(): total = lax.psum(density_sum, ('row', 'col'))  267 us
    psum x1, waiting for transfers between devices, spread(): return lax.psum(block, axis)  112 us
    all_to_all x1, waiting for transfers between devices, on_device(): lax.all_to_all(three_index, 'row', split_axis=0, concat_axis=2, tiled=True)  50.7 us
    dot_general x4, matrix products, pair_terms(): jnp.dot(weighted, partner, precision=lax.Precision.HIGHEST, preferred_ele...  32.2 us
    dot_general x4, matrix products, pair_terms(): lax.dot_general(own_rows, partner, (((1,), (1,)), ((), ())), precision=la...  17.5 us
    dot_general x4, matrix products, pair_terms(): lax.dot_general(weighted, amplitude, (((1,), (1,)), ((), ())), precision=...  12.9 us
  transfers between devices with their start and end apart: 4, of which 3 were waited for; matrix products, arithmetic and copies ran while one was open for 3% of the time, Pallas kernels for 0%

commit v1 on v0

--- a/solution.py
+++ b/solution.py
@@ -76,7 +76,7 @@
         response_sum = response_sum + response
         density_sum = density_sum + virt_density
     returned = lax.all_to_all(response_sum[None], "row", split_axis=2, concat_axis=0, tiled=True)
-    total = lax.psum(density_sum, ("row", "col"))
+    total = lax.psum(lax.psum(density_sum, "col"), "row")
     return (returned, total / (row_count * col_count))
 
 

time: 576 us -> 503 us (0.87)
  waiting for transfers between devices: 430 us -> 357 us
    psum x1 -> x2, waiting for transfers between devices: 267 us -> 194 us  [on_device(): total = lax.psum(lax.psum(density_sum, 'col'), 'row')]
  transfers between devices with their start and end apart: 4 -> 5, of which waited for: 3 -> 4; matrix products, arithmetic and copies ran while one was open for 3% -> 4% of each run, Pallas kernels for 0% -> 0%
where the time goes in v1:
time: 503 us; the launch traced here: 493 us
  waiting for transfers between devices  357 us (71%)
  matrix products  62.6 us (12%)
  local copies, waits for them, and re-layouts  25.2 us (5%)
  between operations  24.6 us (5%)
  starting transfers between devices  15.8 us (3%)
  other arithmetic  8.42 us (2%)
    psum x2, waiting for transfers between devices, on_device(): total = lax.psum(lax.psum(density_sum, 'col'), 'row')  194 us
    psum x1, waiting for transfers between devices, spread(): return lax.psum(block, axis)  112 us
    all_to_all x1, waiting for transfers between devices, on_device(): lax.all_to_all(three_index, 'row', split_axis=0, concat_axis=2, tiled=True)  50.7 us
    dot_general x4, matrix products, pair_terms(): jnp.dot(weighted, partner, precision=lax.Precision.HIGHEST, preferred_ele...  32.2 us
    dot_general x4, matrix products, pair_terms(): lax.dot_general(own_rows, partner, (((1,), (1,)), ((), ())), precision=la...  17.5 us
    dot_general x4, matrix products, pair_terms(): lax.dot_general(weighted, amplitude, (((1,), (1,)), ((), ())), precision=...  12.9 us
  transfers between devices with their start and end apart: 5, of which 4 were waited for; matrix products, arithmetic and copies ran while one was open for 4% of the time, Pallas kernels for 0%

profile of v1, /device:TPU:2, one launch (start us, length us, event | category | flops | bytes accessed | tf_op | source)
XLA Modules:
  0.0 493.4 jit_solution(7626510109737564094)
XLA Ops:
  7.2 2.9 copy.21
  10.1 8.5 %all-to-all-start = ((f32[8,512,128]{1,2,0:T(8,128)}), f32[8,512,128]{1,2,0:T(8,128)S(1)}, u32[]{:S(2)}, u32[]{:S(2)}) async-start(f32[8,512,128]{1,2,0:T(8,128)} %copy.21), calls=%async_computation | async-start | bytes 4194304 | tf_op jit(solution)/shard_map/all_to_all | solution.py:53
  19.1 50.7 %all-to-all-done = f32[8,512,128]{1,2,0:T(8,128)S(1)} async-done(((f32[8,512,128]{1,2,0:T(8,128)}), f32[8,512,128]{1,2,0:T(8,128)S(1)}, u32[]{:S(2)}, u32[]{:S(2)}) %all-to-all-start) | async-done | bytes 2097184 | tf_op jit(solution)/shard_map/all_to_all | solution.py:53
  69.8 3.9 select_bitcast_fusion
  88.2 111.9 %all-reduce.9.cloned.1.call-done = (f32[1,512,1024]{1,2,0:T(8,128)}, f32[1,512,1024]{1,2,0:T(8,128)}, f32[1,512,1024]{1,2,0:T(8,128)}, f32[1,512,1024]{1,2,0:T(8,128)}) async-done(((f32[1,512,1024]{1,2,0:T(8,128)}, f32[1,512,1024]{1,2,0:T(8,128)}, f32[1,512,1024]{1,2,0:T(8,128)}, f32[1,512,1024]{1,2,0:T(8,128)}), (f32[1,512,1024]{1,2,0:T(8,128)}, f32[1,512,1024]{1,2,0:T(8,128)}, f32[1,512,1024]{1,2,0:T(8,128)}, ...) | async-done | bytes 8388624 | tf_op jit(solution)/shard_map/psum | solution.py:15
  205.8 3.5 fusion.2
  209.3 4.6 fusion.6
  213.9 4.9 fusion.10
  218.7 4.5 fusion.14
  223.3 2.7 copy.24
  229.9 9.2 %fusion.8 = f32[512,1024]{1,0:T(8,128)S(1)} fusion(f32[4,512,1024]{1,2,0:T(8,128)} %copy-done.2, s32[]{:T(128)} %bitcast.18, f32[512,512]{1,0:T(8,128)S(1)} %copy-done.5, f32[512]{0:T(512)S(1)} %get-tuple-element.11, f32[512]{0:T(512)S(1)} %copy-done.19, f32[512,512]{0,1:T(8,128)} %copy.25), kind=kOutput, calls=%fused_computation.9 | convolution fusion | flops 3222798336 | bytes 6300160 | tf_op jit(solution)/shard_map/dot_general | solution.py:34
  239.1 8.7 %fusion.4 = f32[512,1024]{1,0:T(8,128)S(1)} fusion(f32[4,512,1024]{1,2,0:T(8,128)} %copy-done.2, s32[]{:T(128)} %bitcast.23, f32[512,512]{1,0:T(8,128)S(1)} %copy-done.3, f32[512]{0:T(512)S(1)} %get-tuple-element.13, f32[512]{0:T(512)S(1)} %copy-done.19, f32[512,512]{0,1:T(8,128)S(1)} %copy-done.13), kind=kOutput, calls=%fused_computation.5 | convolution fusion | flops 3222798336 | bytes 6300160 | tf_op jit(solution)/shard_map/dot_general | solution.py:34
  247.9 7.2 %fusion = f32[512,1024]{1,0:T(8,128)S(1)} fusion(f32[4,512,1024]{1,2,0:T(8,128)S(1)} %bitcast.112, s32[]{:T(128)} %bitcast.28, f32[512,512]{1,0:T(8,128)S(1)} %fusion.2, f32[512]{0:T(512)S(1)} %get-tuple-element.12, f32[512]{0:T(512)S(1)} %copy-done.19, f32[512,512]{0,1:T(8,128)S(1)} %copy-done.11), kind=kOutput, calls=%fused_computation.1 | convolution fusion | flops 3222798336 | bytes 6299652 | tf_op jit(solution)/shard_map/dot_general | solution.py:34
  255.1 7.2 %add_bitcast_fusion = f32[1,512,1024]{2,1,0:T(8,128)S(1)} fusion(f32[512,1024]{1,0:T(8,128)S(1)} %fusion, f32[512,1024]{1,0:T(8,128)S(1)} %fusion.4, f32[512,1024]{1,0:T(8,128)S(1)} %fusion.8, f32[4,512,1024]{1,2,0:T(8,128)S(1)} %bitcast.112, s32[]{:T(128)} %bitcast.13, f32[]{:T(128)} %bitcast.27, f32[]{:T(128)} %bitcast.22, f32[]{:T(128)} %bitcast.17, ...), kind=kOutput, calls=%fused_computation.18 | convolution fusion | flops 3226468352 | bytes 12591124 | tf_op jit(solution)/shard_map/dot_general | solution.py:34
  262.3 3.7 copy.28
  266.0 7.0 %all-to-all-start.1 = ((f32[1,512,1024]{1,0,2:T(1,128)}), f32[1,512,1024]{1,0,2:T(1,128)S(1)}, u32[]{:S(2)}, u32[]{:S(2)}) async-start(f32[1,512,1024]{1,0,2:T(1,128)} %copy.28), calls=%async_computation.1 | async-start | bytes 4194304 | tf_op jit(solution)/shard_map/all_to_all | solution.py:78
  273.3 4.5 convolution_multiply_fusion.3
  277.8 2.5 fusion.28
  280.4 2.5 fusion.27
  282.9 3.5 fusion.26
  286.4 115.4 %all-reduce.5.cloned.1.call-done = f32[512,512]{1,0:T(8,128)} async-done(((f32[512,512]{1,0:T(8,128)}), f32[512,512]{1,0:T(8,128)}) %all-reduce.5.cloned.1.call-update) | async-done | bytes 1048592 | tf_op jit(solution)/shard_map/psum | solution.py:79
  401.9 78.7 %all-reduce.7.cloned.1.call-done = f32[512,512]{1,0:T(8,128)} async-done(((f32[512,512]{1,0:T(8,128)}), f32[512,512]{1,0:T(8,128)}) %all-reduce.7.cloned.1.call-update) | async-done | bytes 1048592 | tf_op jit(solution)/shard_map/psum | solution.py:79
  480.6 2.3 broadcast_multiply_fusion
  482.9 3.6 copy.29
  (70 shorter events, 14.9 us)
Async XLA Ops:
  7.2 11.5 %copy-start = (s32[256,8,16]{0,2,1:T(8,128)S(1)}, s32[256,8,16]{0,2,1:T(8,128)}, u32[]{:S(2)}) copy-start(s32[256,8,16]{0,2,1:T(8,128)} %param.8) | copy-start | bytes 393220
  10.1 59.7 %all-to-all-start = ((f32[8,512,128]{1,2,0:T(8,128)}), f32[8,512,128]{1,2,0:T(8,128)S(1)}, u32[]{:S(2)}, u32[]{:S(2)}) async-start(f32[8,512,128]{1,2,0:T(8,128)} %copy.21), calls=%async_computation | async-start | bytes 4194304 | tf_op jit(solution)/shard_map/all_to_all | solution.py:53
  18.6 181.6 %all-reduce.9.cloned.1.call-start = ((), (), s32[]{:S(2)}) async-start(), calls=%async_computation.4 | async-start | bytes 16777216 | tf_op jit(solution)/shard_map/psum | solution.py:15
  69.8 4.0 copy-start.1
  73.7 6.4 %copy-start.17 = (f32[256]{0:T(256)S(1)}, f32[256]{0:T(256)}, u32[]{:S(2)}) copy-start(f32[256]{0:T(256)} %param.6) | copy-start | bytes 3076
  73.7 12.0 %copy-start.19 = (f32[512]{0:T(512)S(1)}, f32[512]{0:T(512)}, u32[]{:S(2)}) copy-start(f32[512]{0:T(512)} %param.7) | copy-start | bytes 6148
  200.2 2.2 copy-start.10
  205.8 13.0 %copy-start.2 = (f32[4,512,1024]{1,2,0:T(8,128)}, f32[4,512,1024]{1,2,0:T(8,128)S(1)}, u32[]{:S(2)}) copy-start(f32[4,512,1024]{1,2,0:T(8,128)S(1)} %constant_dynamic-update-slice_fusion) | copy-start | bytes 25165828
  223.2 2.7 copy-start.5
  223.2 4.0 copy-start.3
  229.9 9.2 %copy-start.13 = (f32[512,512]{0,1:T(8,128)S(1)}, f32[512,512]{0,1:T(8,128)}, u32[]{:S(2)}) copy-start(f32[512,512]{0,1:T(8,128)} %copy.26) | copy-start | bytes 3145732
  229.9 17.9 %slice-start = ((s8[8388608]{0:T(1024)(128)(4,1)}), s8[4194304]{0:T(1024)(128)(4,1)S(1)}, s32[]{:S(2)}) async-start(s8[8388608]{0:T(1024)(128)(4,1)} %bitcast.111), calls=%async_computation.5 | async-start | bytes 8388608
  239.1 8.7 %slice-start.1 = ((s8[8388608]{0:T(1024)(128)(4,1)}), s8[4194304]{0:T(1024)(128)(4,1)S(1)}, s32[]{:S(2)}) async-start(s8[8388608]{0:T(1024)(128)(4,1)} %bitcast.111), calls=%async_computation.6 | async-start | bytes 8388608
  239.1 8.7 %copy-start.11 = (f32[512,512]{0,1:T(8,128)S(1)}, f32[512,512]{0,1:T(8,128)}, u32[]{:S(2)}) copy-start(f32[512,512]{0,1:T(8,128)} %copy.27) | copy-start | bytes 3145732
  247.9 7.2 %copy-start.7 = (f32[512,512]{1,0:T(8,128)S(1)}, f32[512,512]{1,0:T(8,128)}, u32[]{:S(2)}) copy-start(f32[512,512]{1,0:T(8,128)} %fusion.14) | copy-start | bytes 3145732
  247.9 7.2 %copy-start.16 = (f32[512,512]{0,1:T(8,128)S(1)}, f32[512,512]{0,1:T(8,128)}, u32[]{:S(2)}) copy-start(f32[512,512]{0,1:T(8,128)} %copy.24) | copy-start | bytes 3145732
  266.0 216.9 %all-to-all-start.1 = ((f32[1,512,1024]{1,0,2:T(1,128)}), f32[1,512,1024]{1,0,2:T(1,128)S(1)}, u32[]{:S(2)}, u32[]{:S(2)}) async-start(f32[1,512,1024]{1,0,2:T(1,128)} %copy.28), calls=%async_computation.1 | async-start | bytes 4194304 | tf_op jit(solution)/shard_map/all_to_all | solution.py:78
  273.0 128.9 %all-reduce.5.cloned.1.call-start = ((), (), s32[]{:S(2)}) async-start(), calls=%async_computation.2 | async-start | bytes 2097152 | tf_op jit(solution)/shard_map/psum | solution.py:79
  273.3 4.5 copy-start.6
  273.3 4.5 copy-start.15
  277.8 2.5 copy-start.4
  277.8 2.5 copy-start.14
  280.3 2.5 copy-start.12
  286.4 194.2 %all-reduce.7.cloned.1.call-start = ((), (), s32[]{:S(2)}) async-start(), calls=%async_computation.3 | async-start | bytes 2097152 | tf_op jit(solution)/shard_map/psum | solution.py:79
  (3 other events, 3.9 us)
Sparse Core Ops, SparseCore 0:
  73.9 126.2 all-reduce.8
  286.5 115.3 all-reduce.4
  404.2 76.3 all-reduce.6
